TPU v7x, 32 devices: a whole 2x2x4 slice. The times are simulated.
32 devices in a mesh: ctx: 16 (over z, y, x), ch: 2 (over core).
Axes of the slice: x: 2, y: 2, z: 4, core: 2. Of those that a mesh axis runs over, the one named last changes fastest.
Arguments:
- signal: bfloat16 [4096, 512], P('ctx', 'ch'), may hold values from -6 to 6
- gating: bfloat16 [4096, 512], P('ctx', 'ch'), may hold values from -6 to 6
- filter_taps: bfloat16 [4096], P('ctx'), may hold values from -4 to 4
- cotangent: bfloat16 [4096, 512], P('ctx', 'ch'), may hold values from -6 to 6
Outputs:
- grad_signal: bfloat16 [4096, 512], P('ctx', 'ch')
- grad_gating: bfloat16 [4096, 512], P('ctx', 'ch')
- grad_taps: float32 [4096], P('ctx')
All inputs are finite; a program needn't handle non-finite values.
Results may differ from a plain program's by a relative error of at most 0.0069.
Values may be sent and summed in bfloat16 or wider, within the bound.
A program may use at most 64 MiB of HBM per device.

v0:
```python
import math

import jax
import jax.numpy as jnp
from jax import lax
from jax.sharding import PartitionSpec as P

highest = lax.Precision.HIGHEST


def shifted(block, axis, distance):
    devices = range(lax.axis_size(axis))
    route = [((i - distance) % len(devices), i) for i in devices]
    return lax.ppermute(block, axis, route)


def build_tables(block_len):
    positions = jnp.arange(block_len, dtype=jnp.int32)
    period_len = 2 * block_len
    early_phase = positions[:, None] * positions[None, :] % period_len
    late_phase = (positions[:, None] + block_len) * positions[None, :] % period_len
    early_angle = early_phase.astype(jnp.float32) * (math.pi / block_len)
    late_angle = late_phase.astype(jnp.float32) * (math.pi / block_len)
    weight = jnp.where(positions == 0, 1.0, 2.0).astype(jnp.float32)
    sign_row = jnp.where(positions % 2 == 0, 1.0, -1.0).astype(jnp.float32)
    forward_cos = jnp.cos(early_angle).astype(jnp.bfloat16)
    forward_sin = (-jnp.sin(early_angle)).astype(jnp.bfloat16)
    early_cos = weight[None, :] * jnp.cos(early_angle)
    early_sin = -weight[None, :] * jnp.sin(early_angle)
    late_cos = weight[None, :] * jnp.cos(late_angle)
    late_sin = -weight[None, :] * jnp.sin(late_angle)
    return (forward_cos, forward_sin, early_cos, early_sin, late_cos, late_sin, sign_row)


def block_spectrum(block_data, tables):
    sign_half = tables[6].astype(jnp.bfloat16)
    real_part = jnp.dot(tables[0], block_data, preferred_element_type=jnp.float32)
    imag_part = jnp.dot(tables[1], block_data, preferred_element_type=jnp.float32)
    nyquist = jnp.dot(sign_half[None, :], block_data, preferred_element_type=jnp.float32)
    return (real_part, imag_part, nyquist)


def row_spectrum(row_block, tables):
    sign_half = tables[6].astype(jnp.bfloat16)
    real_part = jnp.dot(row_block, tables[0], preferred_element_type=jnp.float32)
    imag_part = jnp.dot(row_block, tables[1], preferred_element_type=jnp.float32)
    nyquist = jnp.dot(row_block, sign_half[:, None], preferred_element_type=jnp.float32)
    return (real_part, imag_part, nyquist)


def filter_rows_spectrum(row_block, tables):
    g_spec = row_spectrum(row_block, tables)
    flip_row = tables[6][None, :]

    def earlier(member):
        return jnp.concatenate([jnp.zeros_like(member[:1]), member[:-1]], axis=0)

    return (
        earlier(g_spec[0]) + flip_row * g_spec[0],
        earlier(g_spec[1]) + flip_row * g_spec[1],
        earlier(g_spec[2]) + g_spec[2],
    )


def multiply(left_spec, right_spec):
    return (
        left_spec[0] * right_spec[0] - left_spec[1] * right_spec[1],
        left_spec[0] * right_spec[1] + left_spec[1] * right_spec[0],
        left_spec[2] * right_spec[2],
    )


def conj_multiply(left_spec, right_spec):
    return (
        left_spec[0] * right_spec[0] + left_spec[1] * right_spec[1],
        left_spec[0] * right_spec[1] - left_spec[1] * right_spec[0],
        left_spec[2] * right_spec[2],
    )


def add_scaled(totals, increment, factor):
    return tuple(
        (left_part + factor * right_part for left_part, right_part in zip(totals, increment))
    )


def channel_total(spectrum):
    return (
        jnp.sum(spectrum[0], axis=1),
        jnp.sum(spectrum[1], axis=1),
        jnp.sum(spectrum[2], axis=1),
    )


def invert_columns(spectrum, cos_table, sin_table, sign_row, block_len):
    output = jnp.dot(
        cos_table.astype(jnp.bfloat16),
        spectrum[0].astype(jnp.bfloat16),
        preferred_element_type=jnp.float32,
    )
    output = output + jnp.dot(
        sin_table.astype(jnp.bfloat16),
        spectrum[1].astype(jnp.bfloat16),
        preferred_element_type=jnp.float32,
    )
    return (output + sign_row[:, None] * spectrum[2]) / (2.0 * block_len)


def invert_taps(real_part, imag_part, nyquist, cos_table, sin_table, sign_row, block_len):
    output = jnp.dot(cos_table, real_part, precision=highest) + jnp.dot(
        sin_table, imag_part, precision=highest
    )
    return (output + sign_row * nyquist) / (2.0 * block_len)


def following_rows(member):
    return jnp.concatenate([member[1:], jnp.zeros_like(member[:1])], axis=0)


def sequence_layout(signal, grad_mid, cotangent, filter_taps, tables, devices):
    block_len, width_dev = signal.shape
    sign_row = tables[6]
    flip_col = sign_row[:, None]
    my_index = lax.axis_index("ctx")
    zero_cols = jnp.zeros((block_len, width_dev), jnp.float32)
    zero_nyq = jnp.zeros((1, width_dev), jnp.float32)
    blank_spec = (zero_cols, zero_cols, zero_nyq)
    taps_all = lax.all_gather(filter_taps, "ctx", axis=0, tiled=True)
    f_rows = filter_rows_spectrum(taps_all.reshape(devices, block_len), tables)
    own_raw = block_spectrum(grad_mid, tables)
    own_grad = (own_raw[0] * flip_col, own_raw[1] * flip_col, own_raw[2])
    zero_rows = (
        jnp.zeros((devices, block_len), jnp.float32),
        jnp.zeros((devices, block_len), jnp.float32),
        jnp.zeros((devices, 1), jnp.float32),
    )

    def filter_at(index):
        return (
            lax.dynamic_index_in_dim(f_rows[0], index, 0, keepdims=False)[:, None],
            lax.dynamic_index_in_dim(f_rows[1], index, 0, keepdims=False)[:, None],
            lax.dynamic_index_in_dim(f_rows[2], index, 0, keepdims=True),
        )

    def table_step(offset, carried):
        passing, falling, forward, backward, lag_rows = carried
        earlier_ok = (offset <= my_index).astype(jnp.float32)
        later_ok = jnp.logical_or(offset == 0, offset > my_index).astype(jnp.float32)
        later_offset = (devices - offset) % devices
        v_spec = block_spectrum(passing, tables)
        d_raw = block_spectrum(falling, tables)
        d_spec = (d_raw[0] * flip_col, d_raw[1] * flip_col, d_raw[2])
        forward = add_scaled(forward, multiply(filter_at(offset), v_spec), earlier_ok)
        backward = add_scaled(backward, conj_multiply(filter_at(later_offset), d_spec), later_ok)
        lag_term = channel_total(conj_multiply(v_spec, own_grad))
        lag_rows = tuple(
            (
                lax.dynamic_update_index_in_dim(member, earlier_ok * term, offset, 0)
                for member, term in zip(lag_rows, lag_term)
            )
        )
        return (passing, falling, forward, backward, lag_rows)

    def table_turn(offset, carried):
        passing, falling = shifted((carried[0], carried[1]), "ctx", 1)
        return table_step(offset, (passing, falling) + carried[2:])

    carried = table_step(0, (signal, grad_mid, blank_spec, blank_spec, zero_rows))
    carried = lax.fori_loop(1, devices, table_turn, carried)
    forward, backward, lag_rows = (carried[2], carried[3], carried[4])
    summed = (
        lax.psum_scatter(lag_rows[0], "ctx", scatter_dimension=0, tiled=True),
        lax.psum_scatter(lag_rows[1], "ctx", scatter_dimension=0, tiled=True),
        lax.psum_scatter(lag_rows[2], "ctx", scatter_dimension=0, tiled=True),
        lax.psum_scatter(following_rows(lag_rows[0]), "ctx", scatter_dimension=0, tiled=True),
        lax.psum_scatter(following_rows(lag_rows[1]), "ctx", scatter_dimension=0, tiled=True),
        lax.psum_scatter(following_rows(lag_rows[2]), "ctx", scatter_dimension=0, tiled=True),
    )
    lag_own = (summed[0][0], summed[1][0], summed[2][0])
    lag_next = (summed[3][0], summed[4][0], summed[5][0])
    recomputed = invert_columns(forward, tables[4], tables[5], sign_row, block_len)
    grad_gating = (cotangent.astype(jnp.float32) * recomputed).astype(jnp.bfloat16)
    grad_signal = invert_columns(backward, tables[2], tables[3], sign_row, block_len).astype(
        jnp.bfloat16
    )
    return (lag_own, lag_next, grad_signal, grad_gating)


def body(signal, gating, filter_taps, cotangent):
    block_len, width_dev = signal.shape
    devices = lax.axis_size("ctx")
    tables = build_tables(block_len)
    sign_row = tables[6]
    grad_mid = (cotangent.astype(jnp.float32) * gating.astype(jnp.float32)).astype(jnp.bfloat16)
    lag_own, lag_next, grad_signal, grad_gating = sequence_layout(
        signal, grad_mid, cotangent, filter_taps, tables, devices
    )
    totals = lax.psum(
        (lag_own[0], lag_own[1], lag_own[2], lag_next[0], lag_next[1], lag_next[2]), "ch"
    )
    upper_half = invert_taps(
        totals[0], totals[1], totals[2], tables[4], tables[5], sign_row, block_len
    )
    lower_half = invert_taps(
        totals[3], totals[4], totals[5], tables[2], tables[3], sign_row, block_len
    )
    norm_factor = 1.0 / math.sqrt(width_dev * lax.axis_size("ch") * block_len * devices)
    grad_taps = (upper_half + lower_half) * norm_factor
    return (grad_signal, grad_gating, grad_taps)


def solution(mesh):
    in_specs = (P("ctx", "ch"), P("ctx", "ch"), P("ctx"), P("ctx", "ch"))
    out_specs = (P("ctx", "ch"), P("ctx", "ch"), P("ctx"))
    return jax.shard_map(body, mesh=mesh, in_specs=in_specs, out_specs=out_specs, check_vma=False)
```

profile of v0, /device:TPU:0, one launch (start us, length us, event | category | flops | bytes accessed | tf_op | source)
XLA Modules:
  0.0 474.8 jit_solution(15620221570135970930)
XLA Ops:
  8.8 42.4 %all-gather = bf16[16,1,256]{2,1,0:T(2,128)(2,1)S(1)} all-gather(bf16[1,1,256]{2,1,0:T(2,128)(2,1)S(1)} %reshape.228), channel_id=1, replica_groups=mesh['ctx'=16,'ch'=2] {'ctx'}, dimensions={0}, use_global_device_ids=true | all-gather | bytes 8704 | tf_op jit(solution)/shard_map/all_gather | solution.py:128
  61.5 282.1 %while.39 = (s32[]{:T(128)}, bf16[256,256]{1,0:T(8,128)(2,1)S(1)}, bf16[256,256]{1,0:T(8,128)(2,1)S(1)}, f32[256,256]{0,1:T(8,128)S(1)}, f32[256,256]{0,1:T(8,12...) while((s32[]{:T(128)}, bf16[256,256]{1,0:T(8,128)(2,1)S(1)}, ...), condition=%wide.region_7.8_spmd.clone.clone, body=%wide.region_3.7_spmd.clone.clone.sunk | while | flops 140515584 | bytes 6071423 | solution.py:169
  62.5 9.2 %collective-permute-done = bf16[256,256]{1,0:T(8,128)(2,1)S(1)} collective-permute-done((bf16[256,256]{1,0:T(8,128)(2,1)S(1)}, bf16[256,256]{1,0:T(8,128)(2,1)S(1)}, u32[]{:S(2)}, u32[]{:S(2)}) %collective-permute-start) | collective-permute-done | bytes 131104 | tf_op jit(solution)/shard_map/while/body/eval_jaxpr/ppermute | solution.py:14
  72.8 1.4 subtract_reduce_fusion.3
  80.8 9.2 %collective-permute-done = bf16[256,256]{1,0:T(8,128)(2,1)S(1)} collective-permute-done((bf16[256,256]{1,0:T(8,128)(2,1)S(1)}, bf16[256,256]{1,0:T(8,128)(2,1)S(1)}, u32[]{:S(2)}, u32[]{:S(2)}) %collective-permute-start) | collective-permute-done | bytes 131104 | tf_op jit(solution)/shard_map/while/body/eval_jaxpr/ppermute | solution.py:14
  91.1 1.4 subtract_reduce_fusion.3
  99.1 9.2 %collective-permute-done = bf16[256,256]{1,0:T(8,128)(2,1)S(1)} collective-permute-done((bf16[256,256]{1,0:T(8,128)(2,1)S(1)}, bf16[256,256]{1,0:T(8,128)(2,1)S(1)}, u32[]{:S(2)}, u32[]{:S(2)}) %collective-permute-start) | collective-permute-done | bytes 131104 | tf_op jit(solution)/shard_map/while/body/eval_jaxpr/ppermute | solution.py:14
  117.3 9.2 %collective-permute-done = bf16[256,256]{1,0:T(8,128)(2,1)S(1)} collective-permute-done((bf16[256,256]{1,0:T(8,128)(2,1)S(1)}, bf16[256,256]{1,0:T(8,128)(2,1)S(1)}, u32[]{:S(2)}, u32[]{:S(2)}) %collective-permute-start) | collective-permute-done | bytes 131104 | tf_op jit(solution)/shard_map/while/body/eval_jaxpr/ppermute | solution.py:14
  127.7 1.4 subtract_reduce_fusion.3
  135.6 9.2 %collective-permute-done = bf16[256,256]{1,0:T(8,128)(2,1)S(1)} collective-permute-done((bf16[256,256]{1,0:T(8,128)(2,1)S(1)}, bf16[256,256]{1,0:T(8,128)(2,1)S(1)}, u32[]{:S(2)}, u32[]{:S(2)}) %collective-permute-start) | collective-permute-done | bytes 131104 | tf_op jit(solution)/shard_map/while/body/eval_jaxpr/ppermute | solution.py:14
  145.9 1.4 subtract_reduce_fusion.3
  153.9 9.2 %collective-permute-done = bf16[256,256]{1,0:T(8,128)(2,1)S(1)} collective-permute-done((bf16[256,256]{1,0:T(8,128)(2,1)S(1)}, bf16[256,256]{1,0:T(8,128)(2,1)S(1)}, u32[]{:S(2)}, u32[]{:S(2)}) %collective-permute-start) | collective-permute-done | bytes 131104 | tf_op jit(solution)/shard_map/while/body/eval_jaxpr/ppermute | solution.py:14
  172.2 10.0 %collective-permute-done = bf16[256,256]{1,0:T(8,128)(2,1)S(1)} collective-permute-done((bf16[256,256]{1,0:T(8,128)(2,1)S(1)}, bf16[256,256]{1,0:T(8,128)(2,1)S(1)}, u32[]{:S(2)}, u32[]{:S(2)}) %collective-permute-start) | collective-permute-done | bytes 131104 | tf_op jit(solution)/shard_map/while/body/eval_jaxpr/ppermute | solution.py:14
  183.4 1.4 subtract_reduce_fusion.3
  191.4 11.2 %collective-permute-done = bf16[256,256]{1,0:T(8,128)(2,1)S(1)} collective-permute-done((bf16[256,256]{1,0:T(8,128)(2,1)S(1)}, bf16[256,256]{1,0:T(8,128)(2,1)S(1)}, u32[]{:S(2)}, u32[]{:S(2)}) %collective-permute-start) | collective-permute-done | bytes 131104 | tf_op jit(solution)/shard_map/while/body/eval_jaxpr/ppermute | solution.py:14
  203.7 1.4 subtract_reduce_fusion.3
  211.7 11.6 %collective-permute-done = bf16[256,256]{1,0:T(8,128)(2,1)S(1)} collective-permute-done((bf16[256,256]{1,0:T(8,128)(2,1)S(1)}, bf16[256,256]{1,0:T(8,128)(2,1)S(1)}, u32[]{:S(2)}, u32[]{:S(2)}) %collective-permute-start) | collective-permute-done | bytes 131104 | tf_op jit(solution)/shard_map/while/body/eval_jaxpr/ppermute | solution.py:14
  224.4 1.4 subtract_reduce_fusion.3
  232.4 10.8 %collective-permute-done = bf16[256,256]{1,0:T(8,128)(2,1)S(1)} collective-permute-done((bf16[256,256]{1,0:T(8,128)(2,1)S(1)}, bf16[256,256]{1,0:T(8,128)(2,1)S(1)}, u32[]{:S(2)}, u32[]{:S(2)}) %collective-permute-start) | collective-permute-done | bytes 131104 | tf_op jit(solution)/shard_map/while/body/eval_jaxpr/ppermute | solution.py:14
  244.3 1.4 subtract_reduce_fusion.3
  252.3 9.9 %collective-permute-done = bf16[256,256]{1,0:T(8,128)(2,1)S(1)} collective-permute-done((bf16[256,256]{1,0:T(8,128)(2,1)S(1)}, bf16[256,256]{1,0:T(8,128)(2,1)S(1)}, u32[]{:S(2)}, u32[]{:S(2)}) %collective-permute-start) | collective-permute-done | bytes 131104 | tf_op jit(solution)/shard_map/while/body/eval_jaxpr/ppermute | solution.py:14
  263.4 1.4 subtract_reduce_fusion.3
  271.3 9.2 %collective-permute-done = bf16[256,256]{1,0:T(8,128)(2,1)S(1)} collective-permute-done((bf16[256,256]{1,0:T(8,128)(2,1)S(1)}, bf16[256,256]{1,0:T(8,128)(2,1)S(1)}, u32[]{:S(2)}, u32[]{:S(2)}) %collective-permute-start) | collective-permute-done | bytes 131104 | tf_op jit(solution)/shard_map/while/body/eval_jaxpr/ppermute | solution.py:14
  281.6 1.4 subtract_reduce_fusion.3
  289.6 9.2 %collective-permute-done = bf16[256,256]{1,0:T(8,128)(2,1)S(1)} collective-permute-done((bf16[256,256]{1,0:T(8,128)(2,1)S(1)}, bf16[256,256]{1,0:T(8,128)(2,1)S(1)}, u32[]{:S(2)}, u32[]{:S(2)}) %collective-permute-start) | collective-permute-done | bytes 131104 | tf_op jit(solution)/shard_map/while/body/eval_jaxpr/ppermute | solution.py:14
  299.9 1.4 subtract_reduce_fusion.3
  307.9 9.2 %collective-permute-done = bf16[256,256]{1,0:T(8,128)(2,1)S(1)} collective-permute-done((bf16[256,256]{1,0:T(8,128)(2,1)S(1)}, bf16[256,256]{1,0:T(8,128)(2,1)S(1)}, u32[]{:S(2)}, u32[]{:S(2)}) %collective-permute-start) | collective-permute-done | bytes 131104 | tf_op jit(solution)/shard_map/while/body/eval_jaxpr/ppermute | solution.py:14
  318.2 1.4 subtract_reduce_fusion.3
  326.2 9.2 %collective-permute-done = bf16[256,256]{1,0:T(8,128)(2,1)S(1)} collective-permute-done((bf16[256,256]{1,0:T(8,128)(2,1)S(1)}, bf16[256,256]{1,0:T(8,128)(2,1)S(1)}, u32[]{:S(2)}, u32[]{:S(2)}) %collective-permute-start) | collective-permute-done | bytes 131104 | tf_op jit(solution)/shard_map/while/body/eval_jaxpr/ppermute | solution.py:14
  353.7 95.0 %all-reduce.17.cloned.1.call-done = (f32[16,256]{1,0:T(8,128)}, f32[16,256]{1,0:T(8,128)}, f32[16,256]{1,0:T(8,128)}, f32[16,256]{1,0:T(8,128)}, f32[16,1]{0,1:T(1,128)}, /*index=5*/f32[16,1]{0,1:T(1,128)}) async-done(((f32[16,256]{1,0:T(8,128)}, f32[16,256]{1,0:T(8,128)}, f32[16,256]{1,0:T(8,128)}, f32[16,256]{1,0:T(8,128)}, f32[16,1]{0,1:T(1,128)}, /*index=5*/f32[16,1]{0,1:T(1,128)}), ...) | async-done | bytes 65680
  457.7 3.1 all-reduce.14
  466.1 1.9 add_multiply_fusion.1
  (438 shorter events, 143.2 us)
Async XLA Ops:
  7.2 441.5 %all-reduce.17.cloned.1.call-start = ((), (), s32[]{:S(2)}) async-start(), calls=%async_computation | async-start | bytes 133120
  61.6 14.8 %collective-permute-start.1 = (bf16[256,256]{1,0:T(8,128)(2,1)S(1)}, bf16[256,256]{1,0:T(8,128)(2,1)S(1)}, u32[]{:S(2)}, u32[]{:S(2)}) collective-permute-start(bf16[256,256]{1,0:T(8,128)(2,1)S(1)} %get-tuple-element.1174), channel_id=1, source_target_pairs={{30,0},{0,2},{2,4},{4,6},{6,8},{8,10},{10,12},{12,14},{14,16},{16,... | collective-permute-start | bytes 393224 | tf_op jit(solution)/shard_map/while/body/eval_jaxpr/ppermute | solution.py:14
  61.7 10.0 %collective-permute-start = (bf16[256,256]{1,0:T(8,128)(2,1)S(1)}, bf16[256,256]{1,0:T(8,128)(2,1)S(1)}, u32[]{:S(2)}, u32[]{:S(2)}) collective-permute-start(bf16[256,256]{1,0:T(8,128)(2,1)S(1)} %get-tuple-element.1173), channel_id=1, source_target_pairs={{30,0},{0,2},{2,4},{4,6},{6,8},{8,10},{10,12},{12,14},{14,16},{16,... | collective-permute-start | bytes 393224 | tf_op jit(solution)/shard_map/while/body/eval_jaxpr/ppermute | solution.py:14
  79.9 14.8 %collective-permute-start.1 = (bf16[256,256]{1,0:T(8,128)(2,1)S(1)}, bf16[256,256]{1,0:T(8,128)(2,1)S(1)}, u32[]{:S(2)}, u32[]{:S(2)}) collective-permute-start(bf16[256,256]{1,0:T(8,128)(2,1)S(1)} %get-tuple-element.1174), channel_id=1, source_target_pairs={{30,0},{0,2},{2,4},{4,6},{6,8},{8,10},{10,12},{12,14},{14,16},{16,... | collective-permute-start | bytes 393224 | tf_op jit(solution)/shard_map/while/body/eval_jaxpr/ppermute | solution.py:14
  80.0 10.0 %collective-permute-start = (bf16[256,256]{1,0:T(8,128)(2,1)S(1)}, bf16[256,256]{1,0:T(8,128)(2,1)S(1)}, u32[]{:S(2)}, u32[]{:S(2)}) collective-permute-start(bf16[256,256]{1,0:T(8,128)(2,1)S(1)} %get-tuple-element.1173), channel_id=1, source_target_pairs={{30,0},{0,2},{2,4},{4,6},{6,8},{8,10},{10,12},{12,14},{14,16},{16,... | collective-permute-start | bytes 393224 | tf_op jit(solution)/shard_map/while/body/eval_jaxpr/ppermute | solution.py:14
  98.2 14.8 %collective-permute-start.1 = (bf16[256,256]{1,0:T(8,128)(2,1)S(1)}, bf16[256,256]{1,0:T(8,128)(2,1)S(1)}, u32[]{:S(2)}, u32[]{:S(2)}) collective-permute-start(bf16[256,256]{1,0:T(8,128)(2,1)S(1)} %get-tuple-element.1174), channel_id=1, source_target_pairs={{30,0},{0,2},{2,4},{4,6},{6,8},{8,10},{10,12},{12,14},{14,16},{16,... | collective-permute-start | bytes 393224 | tf_op jit(solution)/shard_map/while/body/eval_jaxpr/ppermute | solution.py:14
  98.3 10.0 %collective-permute-start = (bf16[256,256]{1,0:T(8,128)(2,1)S(1)}, bf16[256,256]{1,0:T(8,128)(2,1)S(1)}, u32[]{:S(2)}, u32[]{:S(2)}) collective-permute-start(bf16[256,256]{1,0:T(8,128)(2,1)S(1)} %get-tuple-element.1173), channel_id=1, source_target_pairs={{30,0},{0,2},{2,4},{4,6},{6,8},{8,10},{10,12},{12,14},{14,16},{16,... | collective-permute-start | bytes 393224 | tf_op jit(solution)/shard_map/while/body/eval_jaxpr/ppermute | solution.py:14
  116.5 14.8 %collective-permute-start.1 = (bf16[256,256]{1,0:T(8,128)(2,1)S(1)}, bf16[256,256]{1,0:T(8,128)(2,1)S(1)}, u32[]{:S(2)}, u32[]{:S(2)}) collective-permute-start(bf16[256,256]{1,0:T(8,128)(2,1)S(1)} %get-tuple-element.1174), channel_id=1, source_target_pairs={{30,0},{0,2},{2,4},{4,6},{6,8},{8,10},{10,12},{12,14},{14,16},{16,... | collective-permute-start | bytes 393224 | tf_op jit(solution)/shard_map/while/body/eval_jaxpr/ppermute | solution.py:14
  116.6 10.0 %collective-permute-start = (bf16[256,256]{1,0:T(8,128)(2,1)S(1)}, bf16[256,256]{1,0:T(8,128)(2,1)S(1)}, u32[]{:S(2)}, u32[]{:S(2)}) collective-permute-start(bf16[256,256]{1,0:T(8,128)(2,1)S(1)} %get-tuple-element.1173), channel_id=1, source_target_pairs={{30,0},{0,2},{2,4},{4,6},{6,8},{8,10},{10,12},{12,14},{14,16},{16,... | collective-permute-start | bytes 393224 | tf_op jit(solution)/shard_map/while/body/eval_jaxpr/ppermute | solution.py:14
  134.8 14.8 %collective-permute-start.1 = (bf16[256,256]{1,0:T(8,128)(2,1)S(1)}, bf16[256,256]{1,0:T(8,128)(2,1)S(1)}, u32[]{:S(2)}, u32[]{:S(2)}) collective-permute-start(bf16[256,256]{1,0:T(8,128)(2,1)S(1)} %get-tuple-element.1174), channel_id=1, source_target_pairs={{30,0},{0,2},{2,4},{4,6},{6,8},{8,10},{10,12},{12,14},{14,16},{16,... | collective-permute-start | bytes 393224 | tf_op jit(solution)/shard_map/while/body/eval_jaxpr/ppermute | solution.py:14
  134.8 10.0 %collective-permute-start = (bf16[256,256]{1,0:T(8,128)(2,1)S(1)}, bf16[256,256]{1,0:T(8,128)(2,1)S(1)}, u32[]{:S(2)}, u32[]{:S(2)}) collective-permute-start(bf16[256,256]{1,0:T(8,128)(2,1)S(1)} %get-tuple-element.1173), channel_id=1, source_target_pairs={{30,0},{0,2},{2,4},{4,6},{6,8},{8,10},{10,12},{12,14},{14,16},{16,... | collective-permute-start | bytes 393224 | tf_op jit(solution)/shard_map/while/body/eval_jaxpr/ppermute | solution.py:14
  153.1 14.8 %collective-permute-start.1 = (bf16[256,256]{1,0:T(8,128)(2,1)S(1)}, bf16[256,256]{1,0:T(8,128)(2,1)S(1)}, u32[]{:S(2)}, u32[]{:S(2)}) collective-permute-start(bf16[256,256]{1,0:T(8,128)(2,1)S(1)} %get-tuple-element.1174), channel_id=1, source_target_pairs={{30,0},{0,2},{2,4},{4,6},{6,8},{8,10},{10,12},{12,14},{14,16},{16,... | collective-permute-start | bytes 393224 | tf_op jit(solution)/shard_map/while/body/eval_jaxpr/ppermute | solution.py:14
  153.1 10.0 %collective-permute-start = (bf16[256,256]{1,0:T(8,128)(2,1)S(1)}, bf16[256,256]{1,0:T(8,128)(2,1)S(1)}, u32[]{:S(2)}, u32[]{:S(2)}) collective-permute-start(bf16[256,256]{1,0:T(8,128)(2,1)S(1)} %get-tuple-element.1173), channel_id=1, source_target_pairs={{30,0},{0,2},{2,4},{4,6},{6,8},{8,10},{10,12},{12,14},{14,16},{16,... | collective-permute-start | bytes 393224 | tf_op jit(solution)/shard_map/while/body/eval_jaxpr/ppermute | solution.py:14
  171.3 15.7 %collective-permute-start.1 = (bf16[256,256]{1,0:T(8,128)(2,1)S(1)}, bf16[256,256]{1,0:T(8,128)(2,1)S(1)}, u32[]{:S(2)}, u32[]{:S(2)}) collective-permute-start(bf16[256,256]{1,0:T(8,128)(2,1)S(1)} %get-tuple-element.1174), channel_id=1, source_target_pairs={{30,0},{0,2},{2,4},{4,6},{6,8},{8,10},{10,12},{12,14},{14,16},{16,... | collective-permute-start | bytes 393224 | tf_op jit(solution)/shard_map/while/body/eval_jaxpr/ppermute | solution.py:14
  171.4 10.8 %collective-permute-start = (bf16[256,256]{1,0:T(8,128)(2,1)S(1)}, bf16[256,256]{1,0:T(8,128)(2,1)S(1)}, u32[]{:S(2)}, u32[]{:S(2)}) collective-permute-start(bf16[256,256]{1,0:T(8,128)(2,1)S(1)} %get-tuple-element.1173), channel_id=1, source_target_pairs={{30,0},{0,2},{2,4},{4,6},{6,8},{8,10},{10,12},{12,14},{14,16},{16,... | collective-permute-start | bytes 393224 | tf_op jit(solution)/shard_map/while/body/eval_jaxpr/ppermute | solution.py:14
  190.5 16.9 %collective-permute-start.1 = (bf16[256,256]{1,0:T(8,128)(2,1)S(1)}, bf16[256,256]{1,0:T(8,128)(2,1)S(1)}, u32[]{:S(2)}, u32[]{:S(2)}) collective-permute-start(bf16[256,256]{1,0:T(8,128)(2,1)S(1)} %get-tuple-element.1174), channel_id=1, source_target_pairs={{30,0},{0,2},{2,4},{4,6},{6,8},{8,10},{10,12},{12,14},{14,16},{16,... | collective-permute-start | bytes 393224 | tf_op jit(solution)/shard_map/while/body/eval_jaxpr/ppermute | solution.py:14
  190.6 12.0 %collective-permute-start = (bf16[256,256]{1,0:T(8,128)(2,1)S(1)}, bf16[256,256]{1,0:T(8,128)(2,1)S(1)}, u32[]{:S(2)}, u32[]{:S(2)}) collective-permute-start(bf16[256,256]{1,0:T(8,128)(2,1)S(1)} %get-tuple-element.1173), channel_id=1, source_target_pairs={{30,0},{0,2},{2,4},{4,6},{6,8},{8,10},{10,12},{12,14},{14,16},{16,... | collective-permute-start | bytes 393224 | tf_op jit(solution)/shard_map/while/body/eval_jaxpr/ppermute | solution.py:14
  210.9 17.2 %collective-permute-start.1 = (bf16[256,256]{1,0:T(8,128)(2,1)S(1)}, bf16[256,256]{1,0:T(8,128)(2,1)S(1)}, u32[]{:S(2)}, u32[]{:S(2)}) collective-permute-start(bf16[256,256]{1,0:T(8,128)(2,1)S(1)} %get-tuple-element.1174), channel_id=1, source_target_pairs={{30,0},{0,2},{2,4},{4,6},{6,8},{8,10},{10,12},{12,14},{14,16},{16,... | collective-permute-start | bytes 393224 | tf_op jit(solution)/shard_map/while/body/eval_jaxpr/ppermute | solution.py:14
  210.9 12.4 %collective-permute-start = (bf16[256,256]{1,0:T(8,128)(2,1)S(1)}, bf16[256,256]{1,0:T(8,128)(2,1)S(1)}, u32[]{:S(2)}, u32[]{:S(2)}) collective-permute-start(bf16[256,256]{1,0:T(8,128)(2,1)S(1)} %get-tuple-element.1173), channel_id=1, source_target_pairs={{30,0},{0,2},{2,4},{4,6},{6,8},{8,10},{10,12},{12,14},{14,16},{16,... | collective-permute-start | bytes 393224 | tf_op jit(solution)/shard_map/while/body/eval_jaxpr/ppermute | solution.py:14
  231.5 16.5 %collective-permute-start.1 = (bf16[256,256]{1,0:T(8,128)(2,1)S(1)}, bf16[256,256]{1,0:T(8,128)(2,1)S(1)}, u32[]{:S(2)}, u32[]{:S(2)}) collective-permute-start(bf16[256,256]{1,0:T(8,128)(2,1)S(1)} %get-tuple-element.1174), channel_id=1, source_target_pairs={{30,0},{0,2},{2,4},{4,6},{6,8},{8,10},{10,12},{12,14},{14,16},{16,... | collective-permute-start | bytes 393224 | tf_op jit(solution)/shard_map/while/body/eval_jaxpr/ppermute | solution.py:14
  231.6 11.6 %collective-permute-start = (bf16[256,256]{1,0:T(8,128)(2,1)S(1)}, bf16[256,256]{1,0:T(8,128)(2,1)S(1)}, u32[]{:S(2)}, u32[]{:S(2)}) collective-permute-start(bf16[256,256]{1,0:T(8,128)(2,1)S(1)} %get-tuple-element.1173), channel_id=1, source_target_pairs={{30,0},{0,2},{2,4},{4,6},{6,8},{8,10},{10,12},{12,14},{14,16},{16,... | collective-permute-start | bytes 393224 | tf_op jit(solution)/shard_map/while/body/eval_jaxpr/ppermute | solution.py:14
  251.4 15.6 %collective-permute-start.1 = (bf16[256,256]{1,0:T(8,128)(2,1)S(1)}, bf16[256,256]{1,0:T(8,128)(2,1)S(1)}, u32[]{:S(2)}, u32[]{:S(2)}) collective-permute-start(bf16[256,256]{1,0:T(8,128)(2,1)S(1)} %get-tuple-element.1174), channel_id=1, source_target_pairs={{30,0},{0,2},{2,4},{4,6},{6,8},{8,10},{10,12},{12,14},{14,16},{16,... | collective-permute-start | bytes 393224 | tf_op jit(solution)/shard_map/while/body/eval_jaxpr/ppermute | solution.py:14
  251.5 10.7 %collective-permute-start = (bf16[256,256]{1,0:T(8,128)(2,1)S(1)}, bf16[256,256]{1,0:T(8,128)(2,1)S(1)}, u32[]{:S(2)}, u32[]{:S(2)}) collective-permute-start(bf16[256,256]{1,0:T(8,128)(2,1)S(1)} %get-tuple-element.1173), channel_id=1, source_target_pairs={{30,0},{0,2},{2,4},{4,6},{6,8},{8,10},{10,12},{12,14},{14,16},{16,... | collective-permute-start | bytes 393224 | tf_op jit(solution)/shard_map/while/body/eval_jaxpr/ppermute | solution.py:14
  270.5 14.8 %collective-permute-start.1 = (bf16[256,256]{1,0:T(8,128)(2,1)S(1)}, bf16[256,256]{1,0:T(8,128)(2,1)S(1)}, u32[]{:S(2)}, u32[]{:S(2)}) collective-permute-start(bf16[256,256]{1,0:T(8,128)(2,1)S(1)} %get-tuple-element.1174), channel_id=1, source_target_pairs={{30,0},{0,2},{2,4},{4,6},{6,8},{8,10},{10,12},{12,14},{14,16},{16,... | collective-permute-start | bytes 393224 | tf_op jit(solution)/shard_map/while/body/eval_jaxpr/ppermute | solution.py:14
  270.5 10.0 %collective-permute-start = (bf16[256,256]{1,0:T(8,128)(2,1)S(1)}, bf16[256,256]{1,0:T(8,128)(2,1)S(1)}, u32[]{:S(2)}, u32[]{:S(2)}) collective-permute-start(bf16[256,256]{1,0:T(8,128)(2,1)S(1)} %get-tuple-element.1173), channel_id=1, source_target_pairs={{30,0},{0,2},{2,4},{4,6},{6,8},{8,10},{10,12},{12,14},{14,16},{16,... | collective-permute-start | bytes 393224 | tf_op jit(solution)/shard_map/while/body/eval_jaxpr/ppermute | solution.py:14
  288.8 14.8 %collective-permute-start.1 = (bf16[256,256]{1,0:T(8,128)(2,1)S(1)}, bf16[256,256]{1,0:T(8,128)(2,1)S(1)}, u32[]{:S(2)}, u32[]{:S(2)}) collective-permute-start(bf16[256,256]{1,0:T(8,128)(2,1)S(1)} %get-tuple-element.1174), channel_id=1, source_target_pairs={{30,0},{0,2},{2,4},{4,6},{6,8},{8,10},{10,12},{12,14},{14,16},{16,... | collective-permute-start | bytes 393224 | tf_op jit(solution)/shard_map/while/body/eval_jaxpr/ppermute | solution.py:14
  288.8 10.0 %collective-permute-start = (bf16[256,256]{1,0:T(8,128)(2,1)S(1)}, bf16[256,256]{1,0:T(8,128)(2,1)S(1)}, u32[]{:S(2)}, u32[]{:S(2)}) collective-permute-start(bf16[256,256]{1,0:T(8,128)(2,1)S(1)} %get-tuple-element.1173), channel_id=1, source_target_pairs={{30,0},{0,2},{2,4},{4,6},{6,8},{8,10},{10,12},{12,14},{14,16},{16,... | collective-permute-start | bytes 393224 | tf_op jit(solution)/shard_map/while/body/eval_jaxpr/ppermute | solution.py:14
  307.0 14.8 %collective-permute-start.1 = (bf16[256,256]{1,0:T(8,128)(2,1)S(1)}, bf16[256,256]{1,0:T(8,128)(2,1)S(1)}, u32[]{:S(2)}, u32[]{:S(2)}) collective-permute-start(bf16[256,256]{1,0:T(8,128)(2,1)S(1)} %get-tuple-element.1174), channel_id=1, source_target_pairs={{30,0},{0,2},{2,4},{4,6},{6,8},{8,10},{10,12},{12,14},{14,16},{16,... | collective-permute-start | bytes 393224 | tf_op jit(solution)/shard_map/while/body/eval_jaxpr/ppermute | solution.py:14
  307.1 10.0 %collective-permute-start = (bf16[256,256]{1,0:T(8,128)(2,1)S(1)}, bf16[256,256]{1,0:T(8,128)(2,1)S(1)}, u32[]{:S(2)}, u32[]{:S(2)}) collective-permute-start(bf16[256,256]{1,0:T(8,128)(2,1)S(1)} %get-tuple-element.1173), channel_id=1, source_target_pairs={{30,0},{0,2},{2,4},{4,6},{6,8},{8,10},{10,12},{12,14},{14,16},{16,... | collective-permute-start | bytes 393224 | tf_op jit(solution)/shard_map/while/body/eval_jaxpr/ppermute | solution.py:14
  325.3 14.8 %collective-permute-start.1 = (bf16[256,256]{1,0:T(8,128)(2,1)S(1)}, bf16[256,256]{1,0:T(8,128)(2,1)S(1)}, u32[]{:S(2)}, u32[]{:S(2)}) collective-permute-start(bf16[256,256]{1,0:T(8,128)(2,1)S(1)} %get-tuple-element.1174), channel_id=1, source_target_pairs={{30,0},{0,2},{2,4},{4,6},{6,8},{8,10},{10,12},{12,14},{14,16},{16,... | collective-permute-start | bytes 393224 | tf_op jit(solution)/shard_map/while/body/eval_jaxpr/ppermute | solution.py:14
  325.4 10.0 %collective-permute-start = (bf16[256,256]{1,0:T(8,128)(2,1)S(1)}, bf16[256,256]{1,0:T(8,128)(2,1)S(1)}, u32[]{:S(2)}, u32[]{:S(2)}) collective-permute-start(bf16[256,256]{1,0:T(8,128)(2,1)S(1)} %get-tuple-element.1173), channel_id=1, source_target_pairs={{30,0},{0,2},{2,4},{4,6},{6,8},{8,10},{10,12},{12,14},{14,16},{16,... | collective-permute-start | bytes 393224 | tf_op jit(solution)/shard_map/while/body/eval_jaxpr/ppermute | solution.py:14
  343.6 1.8 copy-start.4
  (8 other events, 6.4 us)
Sparse Core Ops, SparseCore 0:
  346.2 102.4 all-reduce.16
where the time goes:
time: 476 us; the launch traced here: 475 us
  waiting for transfers between devices  240 us (50%)
  matrix products  97.3 us (20%)
  blocking collectives  45.5 us (10%)
  other arithmetic  33.1 us (7%)
  local copies, waits for them, and re-layouts  29.4 us (6%)
  between operations  14.9 us (3%)
  loops' own time  12.5 us (3%)
    ppermute x30, waiting for transfers between devices, shifted(): return lax.ppermute(block, axis, route)  145 us
    unnamed x2, waiting for transfers between devices  95 us
    all_gather x1, blocking collectives, sequence_layout(): taps_all = lax.all_gather(filter_taps, 'ctx', axis=0, tiled=True)  42.4 us
    dot_general x32, matrix products, block_spectrum(): jnp.dot(tables[1], block_data, preferred_element_type=jnp.float32)  42.1 us
    dot_general x32, matrix products, block_spectrum(): jnp.dot(tables[0], block_data, preferred_element_type=jnp.float32)  38.5 us
    reduce_sum x16, other arithmetic, channel_total(): jnp.sum(spectrum[2], axis=1)  19.9 us
    unnamed x34, local copies, waits for them, and re-layouts  15.3 us
    another operation x1, loops' own time, sequence_layout(): carried = lax.fori_loop(1, devices, table_turn, carried)  12.5 us
  transfers between devices with their start and end apart: 31, of which 16 were waited for; matrix products, arithmetic and copies ran while one was open for 17% of the time, Pallas kernels for 0%

commit v1 on v0

v1 whole, which is shorter than its diff:
```python
import functools
import math

import jax
import jax.numpy as jnp
from jax import lax
from jax.experimental import pallas as pl
from jax.experimental.pallas import tpu as pltpu
from jax.sharding import PartitionSpec as P

ROWS = 16
f32 = jnp.float32
bf16 = jnp.bfloat16


def kernel(
    n, cpd, norm,
    signal_ref, gating_ref, taps_ref, cot_ref,
    gs_ref, gg_ref, gt_ref,
    vsend, gsend, xpad, gpad, ysend, bsend, yret, bret,
    taps_all, hpad, toep, acc, xt_ref, mlag, merge, lagsend, lagrecv, lagsum, lagother,
    s_v, r_v, s_g, r_g, s_y, r_y, s_b, r_b, s_t, r_t, s_l, r_l, s_c, r_c,
):
    block, width = signal_ref.shape
    total = n * ROWS
    me = lax.axis_index("ctx")
    mate = 1 - lax.axis_index("ch")
    pieces = lax.axis_size("ch")

    barrier = pltpu.get_barrier_semaphore()

    def greet(d, _):
        pl.semaphore_signal(barrier, inc=1, device_id={"ctx": lax.rem(me + d, n)})
        return 0

    lax.fori_loop(1, n, greet, 0)
    if pieces == 2:
        pl.semaphore_signal(barrier, inc=1, device_id={"ch": mate})

    def split(rows_value, dst):
        if cpd == ROWS:
            dst[...] = rows_value.astype(bf16).reshape(n, ROWS, block)
        else:
            for p in range(n):
                part = rows_value[p * cpd : (p + 1) * cpd]
                pad = jnp.zeros((ROWS - cpd, block), f32)
                dst[p] = jnp.concatenate([part, pad], axis=0).astype(bf16)

    def joined(src):
        if cpd == ROWS:
            return src[...].reshape(width, block).astype(f32)
        for p in range(n):
            merge[p * cpd : (p + 1) * cpd, :] = src[p].astype(f32)[:cpd]
        return merge[...]

    def copy(src, dst, send, recv, p, where):
        return pltpu.make_async_remote_copy(
            src_ref=src, dst_ref=dst, send_sem=send.at[p], recv_sem=recv.at[where],
            device_id={"ctx": p},
        )

    def send_all(src, dst, base, send, recv):
        def step(d, _):
            p = lax.rem(me + d, n)
            copy(src.at[p], dst.at[base + me], send, recv, p, me).start()
            return 0

        lax.fori_loop(1, n, step, 0)

    def wait_recv(src, dst, base, send, recv):
        def step(d, _):
            p = lax.rem(me + n - d, n)
            copy(src.at[p], dst.at[base + p], send, recv, p, p).wait_recv()
            return 0

        lax.fori_loop(1, n, step, 0)

    def wait_send(src, dst, base, send, recv):
        def step(d, _):
            p = lax.rem(me + d, n)
            copy(src.at[p], dst.at[base + me], send, recv, p, me).wait_send()
            return 0

        lax.fori_loop(1, n, step, 0)

    split(signal_ref[...].astype(f32).T, vsend)
    own_taps = taps_ref[...]
    for p in range(n):
        lagrecv[p] = jnp.zeros((1, block), f32)
    taps_send = lagsum
    taps_send[...] = own_taps
    pl.semaphore_wait(barrier, n - 1 + (pieces - 1))

    def taps_step(d, _):
        p = lax.rem(me + d, n)
        copy(taps_send, taps_all.at[me], s_t, r_t, p, me).start()
        return 0

    lax.fori_loop(1, n, taps_step, 0)
    send_all(vsend, xpad, n, s_v, r_v)
    grad_mid = (cot_ref[...].astype(f32) * gating_ref[...].astype(f32)).astype(bf16)
    split(grad_mid.astype(f32).T, gsend)
    send_all(gsend, gpad, 0, s_g, r_g)

    xpad[pl.ds(n + me, 1)] = vsend[pl.ds(me, 1)]
    gpad[pl.ds(me, 1)] = gsend[pl.ds(me, 1)]
    taps_all[pl.ds(me, 1)] = own_taps[None]
    gpad[n:] = jnp.zeros((n, ROWS, block), bf16)
    if n > 16:
        xpad[:n] = jnp.zeros((n, ROWS, block), bf16)

    def taps_wait(d, _):
        p = lax.rem(me + n - d, n)
        copy(taps_send, taps_all.at[p], s_t, r_t, p, p).wait_recv()
        return 0

    lax.fori_loop(1, n, taps_wait, 0)

    def taps_sent(d, _):
        p = lax.rem(me + d, n)
        copy(taps_send, taps_all.at[me], s_t, r_t, p, me).wait_send()
        return 0

    lax.fori_loop(1, n, taps_sent, 0)

    half = block // 2
    hpad[:, :block] = jnp.zeros((1, block), f32)
    for j in range(n):
        hpad[:, (j + 1) * block : (j + 2) * block] = taps_all[j]
    toep[:, :block] = jnp.zeros((half, block), bf16)
    for j in range(1, n + 1):
        window = jnp.broadcast_to(hpad[:, j * block - half : (j + 1) * block], (half, block + half))
        turned = pltpu.roll(window, 0, 1, stride=1, stride_axis=0)
        toep[:, j * block : (j + 1) * block] = turned[:, half:].astype(bf16)

    def at(k):
        return k * block if isinstance(k, int) else pl.multiple_of(k * block, block)

    def table(k):
        upper = toep[:, pl.ds(at(k) + block, block)]
        lower = toep[:, pl.ds(at(k) + half, block)]
        return jnp.concatenate([upper, lower], axis=0)

    def over_blocks(step):
        if n <= 16:
            for k in range(n):
                step(k)
        else:
            lax.fori_loop(0, n, lambda k, _: (step(k), 0)[1], 0)

    nt = (((1,), (1,)), ((), ()))

    def forward_step(k):
        if isinstance(k, int):
            term = jnp.dot(
                xpad[n : 2 * n - k].reshape(total - k * ROWS, block), table(k),
                preferred_element_type=f32,
            ).reshape(n - k, ROWS, block)
            if k == 0:
                acc[...] = term
            else:
                acc[k:] += term
        else:
            acc[...] += jnp.dot(
                xpad[pl.ds(n - k, n)].reshape(total, block), table(k), preferred_element_type=f32
            ).reshape(n, ROWS, block)

    def backward_step(k):
        if isinstance(k, int):
            term = lax.dot_general(
                gpad[k:n].reshape(total - k * ROWS, block), table(k), nt,
                preferred_element_type=f32,
            ).reshape(n - k, ROWS, block)
            if k == 0:
                acc[...] = term
            else:
                acc[: n - k] += term
        else:
            acc[...] += lax.dot_general(
                gpad[pl.ds(k, n)].reshape(total, block), table(k), nt, preferred_element_type=f32
            ).reshape(n, ROWS, block)

    wait_recv(vsend, xpad, n, s_v, r_v)
    if n > 16:
        acc[...] = jnp.zeros((n, ROWS, block), f32)
    over_blocks(forward_step)
    ysend[...] = acc[...].astype(bf16)
    send_all(ysend, yret, 0, s_y, r_y)
    yret[pl.ds(me, 1)] = ysend[pl.ds(me, 1)]
    xt_ref[...] = xpad[n:].reshape(total, block).astype(f32).T.astype(bf16)

    wait_recv(gsend, gpad, 0, s_g, r_g)
    if n > 16:
        acc[...] = jnp.zeros((n, ROWS, block), f32)
    over_blocks(backward_step)
    bsend[...] = acc[...].astype(bf16)
    send_all(bsend, bret, 0, s_b, r_b)
    bret[pl.ds(me, 1)] = bsend[pl.ds(me, 1)]

    def lag_step(k):
        mlag[:, pl.ds(at(k), block)] = jnp.dot(
            xt_ref[...], gpad[pl.ds(k, n)].reshape(total, block), preferred_element_type=f32
        )

    over_blocks(lag_step)
    mlag[:, n * block :] = jnp.zeros((block, block), f32)

    def fold(c):
        start = at(2 * c)
        span = 2 * block + half
        part = mlag[:half, pl.ds(start, span)] + jnp.concatenate(
            [mlag[half:, pl.ds(start + half, 2 * block)], mlag[half:, pl.ds(start + half + 2 * block, half)]],
            axis=1,
        )
        size = half
        while size > 8:
            size //= 2
            part = part[:size] + pltpu.roll(part[size:], span - size, 1)
        while size > 1:
            size //= 2
            part = part + pltpu.roll(pltpu.roll(part, 8 - size, 0), span - size, 1)
        lagsend[2 * c] = part[:1, :block]
        lagsend[2 * c + 1] = part[:1, block : 2 * block]

    if n <= 16:
        for c in range(n // 2):
            fold(c)
    else:
        lax.fori_loop(0, n // 2, lambda c, _: (fold(c), 0)[1], 0)

    send_all(lagsend, lagrecv, 0, s_l, r_l)
    lagrecv[pl.ds(me, 1)] = lagsend[pl.ds(me, 1)]

    wait_recv(ysend, yret, 0, s_y, r_y)
    recomputed = joined(yret).T
    gg_ref[...] = (cot_ref[...].astype(f32) * recomputed).astype(bf16)

    wait_recv(lagsend, lagrecv, 0, s_l, r_l)
    lagsum[...] = jnp.sum(lagrecv[...], axis=0)
    if pieces == 2:
        swap = pltpu.make_async_remote_copy(
            src_ref=lagsum, dst_ref=lagother, send_sem=s_c, recv_sem=r_c, device_id={"ch": mate}
        )
        swap.start()

    wait_recv(bsend, bret, 0, s_b, r_b)
    gs_ref[...] = joined(bret).T.astype(bf16)
    if pieces == 2:
        swap.wait()
        gt_ref[...] = (lagsum[...] + lagother[...]) * norm
    else:
        gt_ref[...] = lagsum[...] * norm
    wait_send(vsend, xpad, n, s_v, r_v)
    wait_send(gsend, gpad, 0, s_g, r_g)
    wait_send(ysend, yret, 0, s_y, r_y)
    wait_send(bsend, bret, 0, s_b, r_b)
    wait_send(lagsend, lagrecv, 0, s_l, r_l)


def body(signal, gating, filter_taps, cotangent):
    block, width = signal.shape
    n = lax.axis_size("ctx")
    cpd = width // n
    norm = 1.0 / math.sqrt(width * lax.axis_size("ch") * block * n)
    chunk = (n, ROWS, block)
    vmem = pl.BlockSpec(memory_space=pltpu.VMEM)
    dma = pltpu.SemaphoreType.DMA
    grad_signal, grad_gating, grad_taps = pl.pallas_call(
        functools.partial(kernel, n, cpd, norm),
        out_shape=(
            jax.ShapeDtypeStruct((block, width), bf16),
            jax.ShapeDtypeStruct((block, width), bf16),
            jax.ShapeDtypeStruct((1, block), f32),
        ),
        in_specs=[vmem] * 4,
        out_specs=(vmem,) * 3,
        scratch_shapes=[
            pltpu.VMEM(chunk, bf16),
            pltpu.VMEM(chunk, bf16),
            pltpu.VMEM((2 * n, ROWS, block), bf16),
            pltpu.VMEM((2 * n, ROWS, block), bf16),
            pltpu.VMEM(chunk, bf16),
            pltpu.VMEM(chunk, bf16),
            pltpu.VMEM(chunk, bf16),
            pltpu.VMEM(chunk, bf16),
            pltpu.VMEM((n, 1, block), f32),
            pltpu.VMEM((1, (n + 1) * block), f32),
            pltpu.VMEM((block // 2, (n + 1) * block), bf16),
            pltpu.VMEM(chunk, f32),
            pltpu.VMEM((block, n * ROWS), bf16),
            pltpu.VMEM((block, (n + 1) * block), f32),
            pltpu.VMEM((width, block), f32),
            pltpu.VMEM((n, 1, block), f32),
            pltpu.VMEM((n, 1, block), f32),
            pltpu.VMEM((1, block), f32),
            pltpu.VMEM((1, block), f32),
        ]
        + [dma((n,))] * 12
        + [dma, dma],
        compiler_params=pltpu.CompilerParams(
            collective_id=0, has_side_effects=True, vmem_limit_bytes=48 * 1024 * 1024
        ),
    )(signal, gating, filter_taps.astype(f32).reshape(1, block), cotangent)
    return (grad_signal, grad_gating, grad_taps.reshape(block))


def solution(mesh):
    in_specs = (P("ctx", "ch"), P("ctx", "ch"), P("ctx"), P("ctx", "ch"))
    out_specs = (P("ctx", "ch"), P("ctx", "ch"), P("ctx"))
    return jax.shard_map(body, mesh=mesh, in_specs=in_specs, out_specs=out_specs, check_vma=False)
```

time: 476 us -> 32.7 us (0.07)
  waiting for transfers between devices: 240 us -> 0 us
  matrix products: 97.3 us -> 0 us
  blocking collectives: 45.5 us -> 0 us
  other arithmetic: 33.1 us -> 0.66 us
  Pallas kernels: 0 us -> 26.6 us
  local copies, waits for them, and re-layouts: 29.4 us -> 4.59 us
  between operations: 14.9 us -> 0.64 us
  loops' own time: 12.5 us -> 0 us
    ppermute x30 -> x0, waiting for transfers between devices: 145 us -> none  [shifted(): return lax.ppermute(block, axis, route)]
    dot_general x107 -> x0, matrix products: 97.3 us -> none  [the longest x32 42.1 us: block_spectrum(): jnp.dot(tables[1], block_data, preferred_element_type=jnp.float32)]
    unnamed x2 -> x0, waiting for transfers between devices: 95 us -> none
    all_gather x1 -> x0, blocking collectives: 42.4 us -> none  [sequence_layout(): taps_all = lax.all_gather(filter_taps, 'ctx', axis=0, tiled=True)]
    pallas_call x0 -> x1, Pallas kernels: none -> 26.6 us  [body(): pl.pallas_call(functools.partial(kernel, n, cpd, norm), out_shape=(jax.Sh...]
    reduce_sum x16 -> x0, other arithmetic: 19.9 us -> none  [channel_total(): jnp.sum(spectrum[2], axis=1)]
    another operation x1 -> x0, loops' own time: 12.5 us -> none  [sequence_layout(): carried = lax.fori_loop(1, devices, table_turn, carried)]
    mul x47 -> x0, other arithmetic: 11.9 us -> none  [the longest x15 9.95 us: add_scaled(): factor * right_part]
  transfers between devices with their start and end apart: 31 -> 0, of which waited for: 16 -> 0; matrix products, arithmetic and copies ran while one was open for 17% -> 0% of each run, Pallas kernels for 0% -> 0%
where the time goes in v1:
time: 32.7 us; the launch traced here: 32.5 us
  Pallas kernels  26.6 us (81%)
  local copies, waits for them, and re-layouts  4.59 us (14%)
  other arithmetic  0.66 us (2%)
  between operations  0.64 us (2%)
    pallas_call x1, Pallas kernels, body(): pl.pallas_call(functools.partial(kernel, n, cpd, norm), out_shape=(jax.Sh...  26.6 us
    unnamed x9, local copies, waits for them, and re-layouts  4.59 us
    reshape x1, other arithmetic, body(): filter_taps.astype(f32).reshape(1, block)  0.66 us

profile of v1, /device:TPU:0, one launch (start us, length us, event | category | flops | bytes accessed | tf_op | source)
XLA Modules:
  0.0 32.5 jit_solution(15873175768075922050)
XLA Ops:
  0.6 0.7 %reshape.17 = f32[256]{0:T(256)S(1)} convert(bf16[256]{0:T(256)(128)(2,1)} %param.6) | non-fusion elementwise | flops 256 | bytes 1536 | tf_op jit(solution)/shard_map/reshape | solution.py:303
  1.3 0.0 copy-start
  1.3 0.9 %copy-done = bf16[256,256]{1,0:T(8,128)(2,1)S(1)} copy-done((bf16[256,256]{1,0:T(8,128)(2,1)S(1)}, bf16[256,256]{1,0:T(8,128)(2,1)}, u32[]{:S(2)}) %copy-start) | copy-done | bytes 131096
  2.2 0.0 copy-start.1
  2.2 0.9 %copy-done.1 = bf16[256,256]{1,0:T(8,128)(2,1)S(1)} copy-done((bf16[256,256]{1,0:T(8,128)(2,1)S(1)}, bf16[256,256]{1,0:T(8,128)(2,1)}, u32[]{:S(2)}) %copy-start.1) | copy-done | bytes 131096
  3.1 0.0 copy-start.2
  3.1 0.9 %copy-done.2 = bf16[256,256]{1,0:T(8,128)(2,1)S(1)} copy-done((bf16[256,256]{1,0:T(8,128)(2,1)S(1)}, bf16[256,256]{1,0:T(8,128)(2,1)}, u32[]{:S(2)}) %copy-start.2) | copy-done | bytes 131096
  4.0 26.6 %shard_map.67 = (bf16[256,256]{1,0:T(8,128)(2,1)S(1)}, bf16[256,256]{1,0:T(8,128)(2,1)S(1)}, f32[1,256]{1,0:T(1,128)S(1)}) custom-call(bf16[256,256]{1,0:T(8,128)(2,1)S(1)} %copy-done, bf16[256,256]{1,0:T(8,128)(2,1)S(1)} %copy-done.1, f32[1,256]{1,0:T(1,128)S(1)} %bitcast.2, bf16[256,256]{1,0:T(8,128)(2,1)S(1)} %copy-done.2), custom_call_target="tpu_custom_call" | custom-call | tf_op jit(solution)/shard_map/pallas_call | solution.py:268
  30.6 0.7 %copy.10 = bf16[256,256]{1,0:T(8,128)(2,1)} copy(bf16[256,256]{1,0:T(8,128)(2,1)S(1)} %get-tuple-element.12) | data formatting | bytes 262144
  31.3 0.7 %copy.11 = bf16[256,256]{1,0:T(8,128)(2,1)} copy(bf16[256,256]{1,0:T(8,128)(2,1)S(1)} %get-tuple-element.13) | data formatting | bytes 262144
  31.9 0.6 %copy.12 = f32[256]{0:T(256)} copy(f32[256]{0:T(256)S(1)} %bitcast.3) | data formatting | bytes 2048
Async XLA Ops:
  1.3 0.9 %copy-start = (bf16[256,256]{1,0:T(8,128)(2,1)S(1)}, bf16[256,256]{1,0:T(8,128)(2,1)}, u32[]{:S(2)}) copy-start(bf16[256,256]{1,0:T(8,128)(2,1)} %signal_ref.1) | copy-start | bytes 393220
  2.2 0.9 %copy-start.1 = (bf16[256,256]{1,0:T(8,128)(2,1)S(1)}, bf16[256,256]{1,0:T(8,128)(2,1)}, u32[]{:S(2)}) copy-start(bf16[256,256]{1,0:T(8,128)(2,1)} %gating_ref.1) | copy-start | bytes 393220
  3.1 0.9 %copy-start.2 = (bf16[256,256]{1,0:T(8,128)(2,1)S(1)}, bf16[256,256]{1,0:T(8,128)(2,1)}, u32[]{:S(2)}) copy-start(bf16[256,256]{1,0:T(8,128)(2,1)} %cot_ref.1) | copy-start | bytes 393220

commit v2 on v1

--- a/solution.py
+++ b/solution.py
@@ -9,17 +9,19 @@
 from jax.sharding import PartitionSpec as P
 
 ROWS = 16
+LONG = 24
 f32 = jnp.float32
 bf16 = jnp.bfloat16
 
 
 def kernel(
     n, cpd, norm,
+    signal_hbm, gating_hbm, taps_hbm, cot_hbm,
+    gs_ref, gg_ref, gt_ref,
     signal_ref, gating_ref, taps_ref, cot_ref,
-    gs_ref, gg_ref, gt_ref,
-    vsend, gsend, xpad, gpad, ysend, bsend, yret, bret,
-    taps_all, hpad, toep, acc, xt_ref, mlag, merge, lagsend, lagrecv, lagsum, lagother,
-    s_v, r_v, s_g, r_g, s_y, r_y, s_b, r_b, s_t, r_t, s_l, r_l, s_c, r_c,
+    vsend, gsend, vrecv, xpad, gpad, ysend, bsend, yret, bret,
+    hpad, toep, acc, xt_ref, mlag, merge, lagsum, lagother,
+    s_v, r_v, s_g, r_g, s_y, r_y, s_b, r_b, s_c, r_c, s_in,
 ):
     block, width = signal_ref.shape
     total = n * ROWS
@@ -28,6 +30,14 @@
     pieces = lax.axis_size("ch")
 
     barrier = pltpu.get_barrier_semaphore()
+    fetches = [
+        pltpu.make_async_copy(src, dst, s_in.at[i])
+        for i, (src, dst) in enumerate(
+            ((signal_hbm, signal_ref), (taps_hbm, taps_ref), (cot_hbm, cot_ref), (gating_hbm, gating_ref))
+        )
+    ]
+    for fetch in fetches:
+        fetch.start()
 
     def greet(d, _):
         pl.semaphore_signal(barrier, inc=1, device_id={"ctx": lax.rem(me + d, n)})
@@ -39,18 +49,18 @@
 
     def split(rows_value, dst):
         if cpd == ROWS:
-            dst[...] = rows_value.astype(bf16).reshape(n, ROWS, block)
+            dst[:, :ROWS, :] = rows_value.astype(bf16).reshape(n, ROWS, block)
         else:
             for p in range(n):
                 part = rows_value[p * cpd : (p + 1) * cpd]
                 pad = jnp.zeros((ROWS - cpd, block), f32)
-                dst[p] = jnp.concatenate([part, pad], axis=0).astype(bf16)
+                dst[p, :ROWS, :] = jnp.concatenate([part, pad], axis=0).astype(bf16)
 
     def joined(src):
         if cpd == ROWS:
-            return src[...].reshape(width, block).astype(f32)
+            return src[:, :ROWS, :].reshape(width, block).astype(f32)
         for p in range(n):
-            merge[p * cpd : (p + 1) * cpd, :] = src[p].astype(f32)[:cpd]
+            merge[p * cpd : (p + 1) * cpd, :] = src[p, :ROWS, :].astype(f32)[:cpd]
         return merge[...]
 
     def copy(src, dst, send, recv, p, where):
@@ -83,50 +93,31 @@
 
         lax.fori_loop(1, n, step, 0)
 
+    fetches[0].wait()
     split(signal_ref[...].astype(f32).T, vsend)
-    own_taps = taps_ref[...]
-    for p in range(n):
-        lagrecv[p] = jnp.zeros((1, block), f32)
-    taps_send = lagsum
-    taps_send[...] = own_taps
+    fetches[1].wait()
+    own_taps = taps_ref[...].astype(f32).reshape(1, block)
+    vsend[:, ROWS:, :] = jnp.broadcast_to(own_taps.astype(bf16)[None], (n, LONG - ROWS, block))
     pl.semaphore_wait(barrier, n - 1 + (pieces - 1))
-
-    def taps_step(d, _):
-        p = lax.rem(me + d, n)
-        copy(taps_send, taps_all.at[me], s_t, r_t, p, me).start()
-        return 0
-
-    lax.fori_loop(1, n, taps_step, 0)
-    send_all(vsend, xpad, n, s_v, r_v)
+    send_all(vsend, vrecv, 0, s_v, r_v)
+    fetches[2].wait()
+    fetches[3].wait()
     grad_mid = (cot_ref[...].astype(f32) * gating_ref[...].astype(f32)).astype(bf16)
     split(grad_mid.astype(f32).T, gsend)
     send_all(gsend, gpad, 0, s_g, r_g)
 
-    xpad[pl.ds(n + me, 1)] = vsend[pl.ds(me, 1)]
+    vrecv[pl.ds(me, 1)] = vsend[pl.ds(me, 1)]
     gpad[pl.ds(me, 1)] = gsend[pl.ds(me, 1)]
-    taps_all[pl.ds(me, 1)] = own_taps[None]
     gpad[n:] = jnp.zeros((n, ROWS, block), bf16)
     if n > 16:
         xpad[:n] = jnp.zeros((n, ROWS, block), bf16)
-
-    def taps_wait(d, _):
-        p = lax.rem(me + n - d, n)
-        copy(taps_send, taps_all.at[p], s_t, r_t, p, p).wait_recv()
-        return 0
-
-    lax.fori_loop(1, n, taps_wait, 0)
-
-    def taps_sent(d, _):
-        p = lax.rem(me + d, n)
-        copy(taps_send, taps_all.at[me], s_t, r_t, p, me).wait_send()
-        return 0
-
-    lax.fori_loop(1, n, taps_sent, 0)
+    wait_recv(vsend, vrecv, 0, s_v, r_v)
+    xpad[n:] = vrecv[:, :ROWS, :]
 
     half = block // 2
     hpad[:, :block] = jnp.zeros((1, block), f32)
     for j in range(n):
-        hpad[:, (j + 1) * block : (j + 2) * block] = taps_all[j]
+        hpad[:, (j + 1) * block : (j + 2) * block] = vrecv[j, ROWS:, :].astype(f32)[:1]
     toep[:, :block] = jnp.zeros((half, block), bf16)
     for j in range(1, n + 1):
         window = jnp.broadcast_to(hpad[:, j * block - half : (j + 1) * block], (half, block + half))
@@ -180,7 +171,6 @@
                 gpad[pl.ds(k, n)].reshape(total, block), table(k), nt, preferred_element_type=f32
             ).reshape(n, ROWS, block)
 
-    wait_recv(vsend, xpad, n, s_v, r_v)
     if n > 16:
         acc[...] = jnp.zeros((n, ROWS, block), f32)
     over_blocks(forward_step)
@@ -190,12 +180,6 @@
     xt_ref[...] = xpad[n:].reshape(total, block).astype(f32).T.astype(bf16)
 
     wait_recv(gsend, gpad, 0, s_g, r_g)
-    if n > 16:
-        acc[...] = jnp.zeros((n, ROWS, block), f32)
-    over_blocks(backward_step)
-    bsend[...] = acc[...].astype(bf16)
-    send_all(bsend, bret, 0, s_b, r_b)
-    bret[pl.ds(me, 1)] = bsend[pl.ds(me, 1)]
 
     def lag_step(k):
         mlag[:, pl.ds(at(k), block)] = jnp.dot(
@@ -219,8 +203,11 @@
         while size > 1:
             size //= 2
             part = part + pltpu.roll(pltpu.roll(part, 8 - size, 0), span - size, 1)
-        lagsend[2 * c] = part[:1, :block]
-        lagsend[2 * c + 1] = part[:1, block : 2 * block]
+        for i in range(2):
+            row = part[:1, i * block : (i + 1) * block]
+            high = row.astype(bf16).astype(f32)
+            tail = jnp.concatenate([high, row - high, jnp.zeros((LONG - ROWS - 2, block), f32)], axis=0)
+            bsend[2 * c + i, ROWS:, :] = tail.astype(bf16)
 
     if n <= 16:
         for c in range(n // 2):
@@ -228,33 +215,46 @@
     else:
         lax.fori_loop(0, n // 2, lambda c, _: (fold(c), 0)[1], 0)
 
-    send_all(lagsend, lagrecv, 0, s_l, r_l)
-    lagrecv[pl.ds(me, 1)] = lagsend[pl.ds(me, 1)]
+    if n > 16:
+        acc[...] = jnp.zeros((n, ROWS, block), f32)
+    over_blocks(backward_step)
+    bsend[:, :ROWS, :] = acc[...].astype(bf16)
+    send_all(bsend, bret, 0, s_b, r_b)
+    bret[pl.ds(me, 1)] = bsend[pl.ds(me, 1)]
 
     wait_recv(ysend, yret, 0, s_y, r_y)
     recomputed = joined(yret).T
     gg_ref[...] = (cot_ref[...].astype(f32) * recomputed).astype(bf16)
 
-    wait_recv(lagsend, lagrecv, 0, s_l, r_l)
-    lagsum[...] = jnp.sum(lagrecv[...], axis=0)
+    wait_recv(bsend, bret, 0, s_b, r_b)
+    lagsum[...] = jnp.sum(jnp.sum(bret[:, ROWS:, :].astype(f32), axis=0), axis=0, keepdims=True)
     if pieces == 2:
         swap = pltpu.make_async_remote_copy(
             src_ref=lagsum, dst_ref=lagother, send_sem=s_c, recv_sem=r_c, device_id={"ch": mate}
         )
         swap.start()
 
-    wait_recv(bsend, bret, 0, s_b, r_b)
     gs_ref[...] = joined(bret).T.astype(bf16)
     if pieces == 2:
         swap.wait()
         gt_ref[...] = (lagsum[...] + lagother[...]) * norm
     else:
         gt_ref[...] = lagsum[...] * norm
-    wait_send(vsend, xpad, n, s_v, r_v)
+    wait_send(vsend, vrecv, 0, s_v, r_v)
     wait_send(gsend, gpad, 0, s_g, r_g)
     wait_send(ysend, yret, 0, s_y, r_y)
     wait_send(bsend, bret, 0, s_b, r_b)
-    wait_send(lagsend, lagrecv, 0, s_l, r_l)
+
+
+def store(gs_in, gg_in, gt_in, gs_out, gg_out, gt_out, sems):
+    copies = [
+        pltpu.make_async_copy(src, dst, sems.at[i])
+        for i, (src, dst) in enumerate(((gs_in, gs_out), (gg_in, gg_out), (gt_in, gt_out)))
+    ]
+    for copy in copies:
+        copy.start()
+    for copy in copies:
+        copy.wait()
 
 
 def body(signal, gating, filter_taps, cotangent):
@@ -263,6 +263,8 @@
     cpd = width // n
     norm = 1.0 / math.sqrt(width * lax.axis_size("ch") * block * n)
     chunk = (n, ROWS, block)
+    longer = (n, LONG, block)
+    hbm = pl.BlockSpec(memory_space=pltpu.HBM)
     vmem = pl.BlockSpec(memory_space=pltpu.VMEM)
     dma = pltpu.SemaphoreType.DMA
     grad_signal, grad_gating, grad_taps = pl.pallas_call(
@@ -272,35 +274,49 @@
             jax.ShapeDtypeStruct((block, width), bf16),
             jax.ShapeDtypeStruct((1, block), f32),
         ),
-        in_specs=[vmem] * 4,
+        in_specs=[hbm] * 4,
         out_specs=(vmem,) * 3,
         scratch_shapes=[
+            pltpu.VMEM((block, width), bf16),
+            pltpu.VMEM((block, width), bf16),
+            pltpu.VMEM((block,), bf16),
+            pltpu.VMEM((block, width), bf16),
+            pltpu.VMEM(longer, bf16),
             pltpu.VMEM(chunk, bf16),
-            pltpu.VMEM(chunk, bf16),
+            pltpu.VMEM(longer, bf16),
             pltpu.VMEM((2 * n, ROWS, block), bf16),
             pltpu.VMEM((2 * n, ROWS, block), bf16),
             pltpu.VMEM(chunk, bf16),
+            pltpu.VMEM(longer, bf16),
             pltpu.VMEM(chunk, bf16),
-            pltpu.VMEM(chunk, bf16),
-            pltpu.VMEM(chunk, bf16),
-            pltpu.VMEM((n, 1, block), f32),
+            pltpu.VMEM(longer, bf16),
             pltpu.VMEM((1, (n + 1) * block), f32),
             pltpu.VMEM((block // 2, (n + 1) * block), bf16),
             pltpu.VMEM(chunk, f32),
             pltpu.VMEM((block, n * ROWS), bf16),
             pltpu.VMEM((block, (n + 1) * block), f32),
             pltpu.VMEM((width, block), f32),
-            pltpu.VMEM((n, 1, block), f32),
-            pltpu.VMEM((n, 1, block), f32),
             pltpu.VMEM((1, block), f32),
             pltpu.VMEM((1, block), f32),
         ]
-        + [dma((n,))] * 12
-        + [dma, dma],
+        + [dma((n,))] * 8
+        + [dma, dma, dma((4,))],
         compiler_params=pltpu.CompilerParams(
-            collective_id=0, has_side_effects=True, vmem_limit_bytes=48 * 1024 * 1024
+            collective_id=0, has_side_effects=True, vmem_limit_bytes=60 * 1024 * 1024
         ),
-    )(signal, gating, filter_taps.astype(f32).reshape(1, block), cotangent)
+    )(signal, gating, filter_taps, cotangent)
+    grad_signal, grad_gating, grad_taps = pl.pallas_call(
+        store,
+        out_shape=(
+            jax.ShapeDtypeStruct((block, width), bf16),
+            jax.ShapeDtypeStruct((block, width), bf16),
+            jax.ShapeDtypeStruct((1, block), f32),
+        ),
+        in_specs=[hbm] * 3,
+        out_specs=(hbm,) * 3,
+        scratch_shapes=[dma((3,))],
+        compiler_params=pltpu.CompilerParams(vmem_limit_bytes=60 * 1024 * 1024),
+    )(grad_signal, grad_gating, grad_taps)
     return (grad_signal, grad_gating, grad_taps.reshape(block))
 
 

time: 32.7 us -> 37.5 us (1.15)
  Pallas kernels: 26.6 us -> 36.7 us
  local copies, waits for them, and re-layouts: 4.59 us -> 0 us
  other arithmetic: 0.66 us -> 0 us
    pallas_call x0 -> x1, Pallas kernels: none -> 9.1 us  [body(): pl.pallas_call(store, out_shape=(jax.ShapeDtypeStruct((block, width), bf1...]
    unnamed x9 -> x0, local copies, waits for them, and re-layouts: 4.59 us -> none
    pallas_call x1, Pallas kernels: 26.6 us -> 27.6 us  [body(): pl.pallas_call(functools.partial(kernel, n, cpd, norm), out_shape=(jax.Sh...]
    reshape x1 -> x0, other arithmetic: 0.66 us -> none  [body(): filter_taps.astype(f32).reshape(1, block)]
where the time goes in v2:
time: 37.5 us; the launch traced here: 37.3 us
  Pallas kernels  36.7 us (98%)
  between operations  0.64 us (2%)
    pallas_call x1, Pallas kernels, body(): pl.pallas_call(functools.partial(kernel, n, cpd, norm), out_shape=(jax.Sh...  27.6 us
    pallas_call x1, Pallas kernels, body(): pl.pallas_call(store, out_shape=(jax.ShapeDtypeStruct((block, width), bf1...  9.1 us

profile of v2, /device:TPU:0, one launch (start us, length us, event | category | flops | bytes accessed | tf_op | source)
XLA Modules:
  0.0 37.3 jit_solution(1452851625368083295)
XLA Ops:
  0.6 27.6 %shard_map.67 = (bf16[256,256]{1,0:T(8,128)(2,1)}, bf16[256,256]{1,0:T(8,128)(2,1)}, f32[1,256]{1,0:T(1,128)}) custom-call(bf16[256,256]{1,0:T(8,128)(2,1)} %signal_hbm.1, bf16[256,256]{1,0:T(8,128)(2,1)} %gating_hbm.1, bf16[256]{0:T(256)(128)(2,1)} %taps_hbm.1, bf16[256,256]{1,0:T(8,128)(2,1)} %cot_hbm.1), custom_call_target="tpu_custom_call" | custom-call | tf_op jit(solution)/shard_map/pallas_call | solution.py:270
  28.2 9.1 %shard_map.68 = (bf16[256,256]{1,0:T(8,128)(2,1)}, bf16[256,256]{1,0:T(8,128)(2,1)}, f32[1,256]{1,0:T(1,128)}) custom-call(bf16[256,256]{1,0:T(8,128)(2,1)} %get-tuple-element.9.gs_in, bf16[256,256]{1,0:T(8,128)(2,1)} %get-tuple-element.10.gg_in, f32[1,256]{1,0:T(1,128)} %get-tuple-element.11.gt_in), custom_call_target="tpu_custom_call" | custom-call | tf_op jit(solution)/shard_map/pallas_call | solution.py:308

commit v3 on v2

--- a/solution.py
+++ b/solution.py
@@ -312,7 +312,7 @@
             jax.ShapeDtypeStruct((block, width), bf16),
             jax.ShapeDtypeStruct((1, block), f32),
         ),
-        in_specs=[hbm] * 3,
+        in_specs=[vmem] * 3,
         out_specs=(hbm,) * 3,
         scratch_shapes=[dma((3,))],
         compiler_params=pltpu.CompilerParams(vmem_limit_bytes=60 * 1024 * 1024),

time: 37.5 us -> 30.1 us (0.80)
  Pallas kernels: 36.7 us -> 29.3 us
    pallas_call x1, Pallas kernels: 9.1 us -> 1.7 us  [body(): pl.pallas_call(store, out_shape=(jax.ShapeDtypeStruct((block, width), bf1...]
where the time goes in v3:
time: 30.1 us; the launch traced here: 29.9 us
  Pallas kernels  29.3 us (97%)
  between operations  0.64 us (2%)
    pallas_call x1, Pallas kernels, body(): pl.pallas_call(functools.partial(kernel, n, cpd, norm), out_shape=(jax.Sh...  27.6 us
    pallas_call x1, Pallas kernels, body(): pl.pallas_call(store, out_shape=(jax.ShapeDtypeStruct((block, width), bf1...  1.7 us

profile of v3, /device:TPU:0, one launch (start us, length us, event | category | flops | bytes accessed | tf_op | source)
XLA Modules:
  0.0 29.9 jit_solution(11871145806946453861)
XLA Ops:
  0.6 27.6 %shard_map.67 = (bf16[256,256]{1,0:T(8,128)(2,1)}, bf16[256,256]{1,0:T(8,128)(2,1)}, f32[1,256]{1,0:T(1,128)}) custom-call(bf16[256,256]{1,0:T(8,128)(2,1)} %signal_hbm.1, bf16[256,256]{1,0:T(8,128)(2,1)} %gating_hbm.1, bf16[256]{0:T(256)(128)(2,1)} %taps_hbm.1, bf16[256,256]{1,0:T(8,128)(2,1)} %cot_hbm.1), custom_call_target="tpu_custom_call" | custom-call | tf_op jit(solution)/shard_map/pallas_call | solution.py:270
  28.2 1.7 %shard_map.68 = (bf16[256,256]{1,0:T(8,128)(2,1)}, bf16[256,256]{1,0:T(8,128)(2,1)}, f32[1,256]{1,0:T(1,128)}) custom-call(bf16[256,256]{1,0:T(8,128)(2,1)} %get-tuple-element.9.gs_in, bf16[256,256]{1,0:T(8,128)(2,1)} %get-tuple-element.10.gg_in, f32[1,256]{1,0:T(1,128)} %get-tuple-element.11.gt_in), custom_call_target="tpu_custom_call" | custom-call | tf_op jit(solution)/shard_map/pallas_call | solution.py:308
